TPU v7x, 32 devices: a whole 2x2x4 slice. The times are simulated.
32 devices in a mesh: row: 4 (over y, core), col: 8 (over z, x).
Axes of the slice: x: 2, y: 2, z: 4, core: 2. Of those that a mesh axis runs over, the one named last changes fastest.
Arguments:
- matrix: float32 [16384, 16384], P('row', 'col'), as said below
Outputs:
- updated: float32 [16384, 16384], P('row', 'col')
- reflectors: float32 [1, 16384, 256], P(None, ('row', 'col'))
- products: float32 [1, 16384, 256], P(None, ('row', 'col'))
Inputs may be any that keep to these rules, and one draw needn't show every extreme that they name: `matrix`: symmetric.
All inputs are finite; a program needn't handle non-finite values.
Results may differ from a plain program's by a relative error of at most 0.0003.
Values sent between devices are 32-bit elements; how exact they have to be, the bound alone decides.
A program may use at most 192 MiB of HBM per device.

v0:
```python
import jax
import jax.numpy as jnp
from jax import lax
from jax.sharding import PartitionSpec as P

NB = 256
leaf_width = 16


def spread(value, axis, source):
    kept = jnp.where(lax.axis_index(axis) == source, value, 0).astype(value.dtype)
    return lax.psum(kept, axis)


def matmul(left, right):
    return jnp.dot(left, right, precision=lax.Precision.HIGHEST, preferred_element_type=jnp.float32)


def lu_signed(square):
    order_n = square.shape[0]
    width = min(leaf_width, order_n)
    all_ids = jnp.arange(order_n)
    panel_ids = jnp.arange(width)
    work_mat = square
    sign_vec = jnp.zeros((order_n,), jnp.float32)
    for first in range(0, order_n, width):
        panel = work_mat[:, first : first + width]

        def leaf_step(local_idx, state, first=first):
            panel, sign_vec = state
            pivot_idx = first + local_idx
            column = lax.dynamic_slice_in_dim(panel, local_idx, 1, 1)[:, 0]
            raw_pivot = column[pivot_idx]
            sign_now = jnp.where(raw_pivot >= 0, 1.0, -1.0).astype(jnp.float32)
            pivot_val = raw_pivot + sign_now
            lower_col = jnp.where(all_ids > pivot_idx, column / pivot_val, 0.0)
            upper_row = jnp.where(panel_ids > local_idx, panel[pivot_idx, :], 0.0)
            panel = panel - lower_col[:, None] * upper_row[None, :]
            kept = jnp.where(
                all_ids > pivot_idx, lower_col, jnp.where(all_ids == pivot_idx, pivot_val, column)
            )
            panel = lax.dynamic_update_slice_in_dim(panel, kept[:, None], local_idx, 1)
            sign_vec = sign_vec.at[pivot_idx].set(sign_now)
            return (panel, sign_vec)

        panel, sign_vec = lax.fori_loop(0, width, leaf_step, (panel, sign_vec))
        work_mat = work_mat.at[:, first : first + width].set(panel)
        after = first + width
        if after < order_n:
            diag_lower = jnp.tril(panel[first:after], -1) + jnp.eye(width, dtype=jnp.float32)
            upper_right = jax.scipy.linalg.solve_triangular(
                diag_lower, work_mat[first:after, after:], lower=True, unit_diagonal=True
            )
            trailing = work_mat[after:, after:] - matmul(panel[after:], upper_right)
            work_mat = work_mat.at[first:after, after:].set(upper_right)
            work_mat = work_mat.at[after:, after:].set(trailing)
    unit_lower = jnp.tril(work_mat, -1) + jnp.eye(order_n, dtype=jnp.float32)
    return (unit_lower, jnp.triu(work_mat), sign_vec)


def body(matrix):
    row_count, col_count = matrix.shape
    row_index = lax.axis_index("row")
    col_index = lax.axis_index("col")
    col_devices = lax.axis_size("col")
    share_rows = row_count // col_devices
    row_ids = row_index * row_count + jnp.arange(row_count)
    owner_row = col_index * col_count // row_count
    owner_offset = col_index * col_count % row_count
    current = matrix
    row_start = NB
    panel_cols = lax.slice_in_dim(current, 0, NB, axis=1)
    panel_cols = spread(panel_cols, "col", 0)
    panel_cols = jnp.where((row_ids >= row_start)[:, None], panel_cols, 0.0)
    gram_sum = lax.psum(matmul(panel_cols.T, panel_cols), "row")
    chol_low = jnp.linalg.cholesky(gram_sum)
    q_basis = jax.scipy.linalg.solve_triangular(chol_low, panel_cols.T, lower=True).T
    top_block = spread(q_basis[row_start : row_start + NB], "row", 0)
    unit_lower, upper_tri, sign_diag = lu_signed(top_block)
    solved = jax.scipy.linalg.solve_triangular(upper_tri.T, q_basis.T, lower=True).T
    rel_pos = row_ids - row_start
    in_top = (rel_pos >= 0) & (rel_pos < NB)
    lower_rows = jnp.take(unit_lower, jnp.clip(rel_pos, 0, NB - 1), axis=0)
    refl = jnp.where(in_top[:, None], lower_rows, jnp.where((rel_pos < 0)[:, None], 0.0, solved))
    scaled = upper_tri * sign_diag[None, :]
    t_factor = jax.scipy.linalg.solve_triangular(
        unit_lower, scaled.T, lower=True, unit_diagonal=True
    ).T
    own_slice = lax.dynamic_slice_in_dim(refl, owner_offset, col_count, 0)
    refl_cols = spread(own_slice, "row", owner_row)
    x_rows = lax.psum(matmul(current, matmul(refl_cols, t_factor)), "col")
    inner_prod = lax.psum(matmul(refl.T, x_rows), "row")
    correction = matmul(t_factor.T, inner_prod)
    w_rows = x_rows - 0.5 * matmul(refl, correction)
    x_cols = lax.psum(matmul(current.T, matmul(refl, t_factor)), "row")
    w_cols = x_cols - 0.5 * matmul(refl_cols, correction)
    left_pair = jnp.concatenate([refl, w_rows], axis=1)
    right_pair = jnp.concatenate([w_cols, refl_cols], axis=1)
    current = current - matmul(left_pair, right_pair.T)
    all_refl = [lax.dynamic_slice_in_dim(refl, col_index * share_rows, share_rows, 0)]
    all_prod = [lax.dynamic_slice_in_dim(w_rows, col_index * share_rows, share_rows, 0)]
    return (current, jnp.stack(all_refl), jnp.stack(all_prod))


def solution(mesh):
    return jax.shard_map(
        body,
        mesh=mesh,
        in_specs=(P("row", "col"),),
        out_specs=(P("row", "col"), P(None, ("row", "col"), None), P(None, ("row", "col"), None)),
        check_vma=False,
    )
```

profile of v0, /device:TPU:0, one launch (start us, length us, event | category | flops | bytes accessed | tf_op | source)
XLA Modules:
  0.0 1536.2 jit_solution(7830137127578075882)
XLA Ops:
  7.2 4.5 slice_select_fusion
  12.6 158.8 %all-reduce.9.cloned.1.call-done = f32[4096,256]{1,0:T(8,128)} async-done(((f32[4096,256]{1,0:T(8,128)}), f32[4096,256]{1,0:T(8,128)}) %all-reduce.9.cloned.1.call-update) | async-done | bytes 4194320 | tf_op jit(solution)/shard_map/psum | solution.py:12
  171.4 12.2 fusion.89
  183.8 3.9 select_bitcast_fusion
  187.8 27.3 %all-reduce.11.cloned.1.call-done = f32[256,256]{0,1:T(8,128)} async-done(((f32[256,256]{0,1:T(8,128)}), f32[256,256]{0,1:T(8,128)}) %all-reduce.11.cloned.1.call-update) | async-done | bytes 262160 | tf_op jit(solution)/shard_map/psum | solution.py:75
  217.1 11.7 cholesky.50
  228.9 9.8 custom-call.78
  239.2 11.7 cholesky.105
  253.1 4.0 while.404
  257.0 19.9 %custom-call.96 = f32[2,128,128]{1,2,0:T(8,128)S(1)} custom-call(f32[2,128,128]{2,1,0:T(8,128)S(1)} %get-tuple-element.3807), custom_call_target="InvertDiagBlocksLowerTriangular" | custom-call | tf_op jit(solution)/shard_map/jit(_solve_triangular)/triangular_solve | solution.py:77
  276.9 3.7 fusion.92
  280.6 4.8 convolution_subtract_fusion.2
  287.2 3.5 fusion.110
  303.7 21.8 %all-reduce.13.cloned.1.call-done = f32[256,256]{1,0:T(8,128)} async-done(((f32[256,256]{1,0:T(8,128)}), f32[256,256]{1,0:T(8,128)}) %all-reduce.13.cloned.1.call-update) | async-done | bytes 262160 | tf_op jit(solution)/shard_map/psum | solution.py:12
  326.5 37.1 %while.388 = (s32[]{:T(128)}, f32[256,16]{0,1:T(8,128)S(1)}, f32[256]{0:T(256)S(1)}, s32[]{:T(128)}, s32[]{:T(128)}, /*index=5*/s32[]{:T(128)}, s32[]{:T(128)}, f32[]{:T(128)}, f32[]{:T(128)}, f32[]{:T(128)}) while((s32[]{:T(128)}, f32[256,16]{0,1:T(8,128)S(1)}, f32[256]{0:T(256)S(1)}, s32[]{:T(128)}, s32[]{:T(128)}, ...), condition=%wide.region_9.11_spmd.clone.clone, body=%wide.region_8.10_spmd.clone.clone.sunk | while | flops 9771 | bytes 75169 | solution.py:46
  368.2 2.8 dynamic-slice_select_fusion.1
  372.4 3.4 scatter.220
  375.9 2.4 scatter.221
  379.3 37.1 %while.389 = (s32[]{:T(128)}, f32[256,16]{0,1:T(8,128)S(1)}, f32[256]{0:T(256)S(1)}, s32[]{:T(128)}, s32[]{:T(128)}, /*index=5*/s32[]{:T(128)}, s32[]{:T(128)}, ...) while((s32[]{:T(128)}, f32[256,16]{0,1:T(8,128)S(1)}, ...), condition=%wide.region_13.15_spmd.clone.clone, body=%wide.region_12.14_spmd.clone.clone.sunk | while | flops 9775 | bytes 74215 | solution.py:46
  423.8 2.3 scatter.225
  426.0 2.4 scatter.226
  429.5 37.1 %while.390 = (s32[]{:T(128)}, f32[256,16]{0,1:T(8,128)S(1)}, f32[256]{0:T(256)S(1)}, s32[]{:T(128)}, s32[]{:T(128)}, /*index=5*/s32[]{:T(128)}, s32[]{:T(128)}, ...) while((s32[]{:T(128)}, f32[256,16]{0,1:T(8,128)S(1)}, ...), condition=%wide.region_16.18_spmd.clone.clone, body=%wide.region_15.17_spmd.clone.clone.sunk | while | flops 9775 | bytes 74215 | solution.py:46
  473.8 2.3 scatter.230
  476.1 2.3 scatter.231
  479.5 37.1 %while.391 = (s32[]{:T(128)}, f32[256,16]{0,1:T(8,128)S(1)}, f32[256]{0:T(256)S(1)}, s32[]{:T(128)}, s32[]{:T(128)}, /*index=5*/s32[]{:T(128)}, s32[]{:T(128)}, ...) while((s32[]{:T(128)}, f32[256,16]{0,1:T(8,128)S(1)}, ...), condition=%wide.region_19.21_spmd.clone.clone, body=%wide.region_18.20_spmd.clone.clone.sunk | while | flops 9775 | bytes 74215 | solution.py:46
  523.8 2.2 scatter.235
  526.0 2.3 scatter.237
  529.4 37.1 %while.392 = (s32[]{:T(128)}, f32[256,16]{0,1:T(8,128)S(1)}, f32[256]{0:T(256)S(1)}, s32[]{:T(128)}, s32[]{:T(128)}, /*index=5*/s32[]{:T(128)}, s32[]{:T(128)}, ...) while((s32[]{:T(128)}, f32[256,16]{0,1:T(8,128)S(1)}, ...), condition=%wide.region_22.24_spmd.clone.clone, body=%wide.region_21.23_spmd.clone.clone.sunk | while | flops 9775 | bytes 74215 | solution.py:46
  573.6 2.2 scatter.241
  575.9 2.2 scatter.242
  579.1 37.1 %while.393 = (s32[]{:T(128)}, f32[256,16]{0,1:T(8,128)S(1)}, f32[256]{0:T(256)S(1)}, s32[]{:T(128)}, s32[]{:T(128)}, /*index=5*/s32[]{:T(128)}, s32[]{:T(128)}, ...) while((s32[]{:T(128)}, f32[256,16]{0,1:T(8,128)S(1)}, ...), condition=%wide.region_25.27_spmd.clone.clone, body=%wide.region_24.26_spmd.clone.clone.sunk | while | flops 9775 | bytes 74215 | solution.py:46
  623.5 2.3 scatter.246
  625.7 2.2 scatter.247
  629.0 37.1 %while.394 = (s32[]{:T(128)}, f32[256,16]{0,1:T(8,128)S(1)}, f32[256]{0:T(256)S(1)}, s32[]{:T(128)}, s32[]{:T(128)}, /*index=5*/s32[]{:T(128)}, s32[]{:T(128)}, ...) while((s32[]{:T(128)}, f32[256,16]{0,1:T(8,128)S(1)}, ...), condition=%wide.region_28.30_spmd.clone.clone, body=%wide.region_27.29_spmd.clone.clone.sunk | while | flops 9775 | bytes 74215 | solution.py:46
  673.3 2.4 scatter.251
  675.7 2.1 scatter.252
  678.9 37.1 %while.395 = (s32[]{:T(128)}, f32[256,16]{0,1:T(8,128)S(1)}, f32[256]{0:T(256)S(1)}, s32[]{:T(128)}, s32[]{:T(128)}, /*index=5*/s32[]{:T(128)}, s32[]{:T(128)}, ...) while((s32[]{:T(128)}, f32[256,16]{0,1:T(8,128)S(1)}, ...), condition=%wide.region_31.33_spmd.clone.clone, body=%wide.region_30.32_spmd.clone.clone.sunk | while | flops 9775 | bytes 74215 | solution.py:46
  724.0 37.1 %while.396 = (s32[]{:T(128)}, f32[256,16]{0,1:T(8,128)S(1)}, f32[256]{0:T(256)S(1)}, s32[]{:T(128)}, s32[]{:T(128)}, /*index=5*/s32[]{:T(128)}, s32[]{:T(128)}, ...) while((s32[]{:T(128)}, f32[256,16]{0,1:T(8,128)S(1)}, ...), condition=%wide.region_34.36_spmd.clone.clone, body=%wide.region_33.35_spmd.clone.clone.sunk | while | flops 9775 | bytes 74215 | solution.py:46
  766.7 37.1 %while.397 = (s32[]{:T(128)}, f32[256,16]{0,1:T(8,128)S(1)}, f32[256]{0:T(256)S(1)}, s32[]{:T(128)}, s32[]{:T(128)}, /*index=5*/s32[]{:T(128)}, s32[]{:T(128)}, ...) while((s32[]{:T(128)}, f32[256,16]{0,1:T(8,128)S(1)}, ...), condition=%wide.region_37.39_spmd.clone.clone, body=%wide.region_36.38_spmd.clone.clone.sunk | while | flops 9775 | bytes 74215 | solution.py:46
  809.5 37.1 %while.398 = (s32[]{:T(128)}, f32[256,16]{0,1:T(8,128)S(1)}, f32[256]{0:T(256)S(1)}, s32[]{:T(128)}, s32[]{:T(128)}, /*index=5*/s32[]{:T(128)}, s32[]{:T(128)}, ...) while((s32[]{:T(128)}, f32[256,16]{0,1:T(8,128)S(1)}, ...), condition=%wide.region_40.42_spmd.clone.clone, body=%wide.region_39.41_spmd.clone.clone.sunk | while | flops 9775 | bytes 74215 | solution.py:46
  852.3 37.1 %while.399 = (s32[]{:T(128)}, f32[256,16]{0,1:T(8,128)S(1)}, f32[256]{0:T(256)S(1)}, s32[]{:T(128)}, s32[]{:T(128)}, /*index=5*/s32[]{:T(128)}, s32[]{:T(128)}, ...) while((s32[]{:T(128)}, f32[256,16]{0,1:T(8,128)S(1)}, ...), condition=%wide.region_43.45_spmd.clone.clone, body=%wide.region_42.44_spmd.clone.clone.sunk | while | flops 9775 | bytes 74215 | solution.py:46
  894.9 37.1 %while.400 = (s32[]{:T(128)}, f32[256,16]{0,1:T(8,128)S(1)}, f32[256]{0:T(256)S(1)}, s32[]{:T(128)}, s32[]{:T(128)}, /*index=5*/s32[]{:T(128)}, s32[]{:T(128)}, ...) while((s32[]{:T(128)}, f32[256,16]{0,1:T(8,128)S(1)}, ...), condition=%wide.region_46.48_spmd.clone.clone, body=%wide.region_45.47_spmd.clone.clone.sunk | while | flops 9775 | bytes 74215 | solution.py:46
  937.6 37.1 %while.401 = (s32[]{:T(128)}, f32[256,16]{0,1:T(8,128)S(1)}, f32[256]{0:T(256)S(1)}, s32[]{:T(128)}, s32[]{:T(128)}, /*index=5*/s32[]{:T(128)}, s32[]{:T(128)}, ...) while((s32[]{:T(128)}, f32[256,16]{0,1:T(8,128)S(1)}, ...), condition=%wide.region_49.51_spmd.clone.clone, body=%wide.region_48.50_spmd.clone.clone.sunk | while | flops 9775 | bytes 74215 | solution.py:46
  980.2 37.1 %while.402 = (s32[]{:T(128)}, f32[256,16]{0,1:T(8,128)S(1)}, f32[256]{0:T(256)S(1)}, s32[]{:T(128)}, s32[]{:T(128)}, /*index=5*/s32[]{:T(128)}, s32[]{:T(128)}, ...) while((s32[]{:T(128)}, f32[256,16]{0,1:T(8,128)S(1)}, ...), condition=%wide.region_52.54_spmd.clone.clone, body=%wide.region_51.53_spmd.clone.clone.sunk | while | flops 9775 | bytes 74215 | solution.py:46
  1022.6 37.1 %while.403 = (s32[]{:T(128)}, f32[256,16]{0,1:T(8,128)S(1)}, f32[256]{0:T(256)S(1)}, s32[]{:T(128)}, s32[]{:T(128)}, /*index=5*/s32[]{:T(128)}, s32[]{:T(128)}, ...) while((s32[]{:T(128)}, f32[256,16]{0,1:T(8,128)S(1)}, ...), condition=%wide.region_54.56_spmd.clone.clone, body=%wide.region_53.55_spmd.clone.clone.sunk | while | flops 9775 | bytes 74215 | solution.py:46
  1060.9 16.1 %gather_fusion = f32[4096,256]{1,0:T(8,128)} fusion(f32[256,256]{1,0:T(8,128)S(1)} %get-tuple-element.4059, s32[4096]{0:T(1024)S(1)} %broadcast_clamp_fusion), kind=kCustom, calls=%fused_computation | custom fusion | bytes 8404992 | tf_op jit(solution)/shard_map/jit(_take)/gather | solution.py:83
  1077.0 5.6 copy.109
  1082.6 4.2 while.405
  1086.9 19.9 %custom-call.97 = f32[2,128,128]{1,2,0:T(8,128)S(1)} custom-call(f32[2,128,128]{2,1,0:T(8,128)S(1)} %get-tuple-element.3808), custom_call_target="InvertDiagBlocksLowerTriangular" | custom-call | tf_op jit(solution)/shard_map/jit(_solve_triangular)/triangular_solve | solution.py:80
  1108.8 3.6 convolution_subtract_fusion.1
  1118.9 4.5 while.387
  1123.4 19.7 %custom-call.94 = f32[2,128,128]{1,2,0:T(8,128)S(1)} custom-call(f32[2,128,128]{2,1,0:T(8,128)S(1)} %get-tuple-element.3432), custom_call_target="InvertDiagBlocksLowerTriangular" | custom-call | tf_op jit(solution)/shard_map/jit(_solve_triangular)/triangular_solve | solution.py:86
  1144.1 26.3 %all-reduce.15.cloned.1.call-done = f32[2048,256]{0,1:T(8,128)} async-done(((f32[2048,256]{0,1:T(8,128)}), f32[2048,256]{0,1:T(8,128)}) %all-reduce.15.cloned.1.call-update) | async-done | bytes 2097168 | tf_op jit(solution)/shard_map/psum | solution.py:12
  1170.4 5.0 fusion.101
  1175.4 58.3 %convolution_bitcast_fusion = f32[4096,256]{0,1:T(8,128)} fusion(f32[2048,256]{1,0:T(8,128)S(1)} %fusion.101, f32[4096,2048]{1,0:T(8,128)} %param.159), kind=kOutput, calls=%fused_computation.205 | convolution fusion | flops 25769803776 | bytes 39845888 | tf_op jit(solution)/shard_map/dot_general | solution.py:16
  1233.8 8.5 fusion.99
  1242.3 33.1 %convolution_bitcast_fusion.1 = f32[2048,256]{0,1:T(8,128)} fusion(f32[4096,256]{1,0:T(8,128)S(1)} %fusion.99, f32[4096,2048]{1,0:T(8,128)} %param.159), kind=kOutput, calls=%fused_computation.221 | convolution fusion | flops 25769803776 | bytes 39845888 | tf_op jit(solution)/shard_map/dot_general | solution.py:16
  1275.4 115.0 %all-reduce.17.cloned.1.call-done = f32[4096,256]{0,1:T(8,128)} async-done(((f32[4096,256]{0,1:T(8,128)}), f32[4096,256]{0,1:T(8,128)}) %all-reduce.17.cloned.1.call-update) | async-done | bytes 4194320 | tf_op jit(solution)/shard_map/psum | solution.py:91
  1390.4 7.7 fusion.222
  1400.2 52.7 %all-reduce.19.cloned.1.call-done = (f32[256,256]{1,0:T(8,128)}, f32[2048,256]{0,1:T(8,128)}) async-done(((f32[256,256]{1,0:T(8,128)}, f32[2048,256]{0,1:T(8,128)}), (f32[256,256]{1,0:T(8,128)}, f32[2048,256]{0,1:T(8,128)})) %all-reduce.19.cloned.1.call-update) | async-done | bytes 2359312 | tf_op jit(solution)/shard_map/psum | solution.py:92
  1454.3 8.2 fusion.83
  1462.5 2.0 copy-done.2
  1465.5 3.8 fusion.91
  1469.3 59.8 %convolution_subtract_fusion = f32[4096,2048]{1,0:T(8,128)} fusion(f32[4096,2048]{1,0:T(8,128)} %param.159, f32[4096,256]{0,1:T(8,128)} %copy-done.2, f32[4096,256]{0,1:T(8,128)S(1)} %copy-done.1, f32[2048,256]{0,1:T(8,128)S(1)} %copy-done.5, f32[2048,256]{0,1:T(8,128)S(1)} %fusion.91), kind=kOutput, calls=%fused_computation.199 | convolution fusion | flops 51551141888 | bytes 79691776 | tf_op jit(solution)/shard_map/dot_general | solution.py:16
  (2313 shorter events, 403.3 us)
Async XLA Ops:
  7.2 164.2 %all-reduce.9.cloned.1.call-start = ((), (), s32[]{:S(2)}) async-start(), calls=%async_computation | async-start | bytes 8388608 | tf_op jit(solution)/shard_map/psum | solution.py:12
  11.7 203.3 %all-reduce.11.cloned.1.call-start = ((), (), s32[]{:S(2)}) async-start(), calls=%async_computation.1 | async-start | bytes 524288 | tf_op jit(solution)/shard_map/psum | solution.py:75
  183.6 141.9 %all-reduce.13.cloned.1.call-start = ((), (), s32[]{:S(2)}) async-start(), calls=%async_computation.2 | async-start | bytes 524288 | tf_op jit(solution)/shard_map/psum | solution.py:12
  276.9 3.7 copy-start.7
  287.2 4.9 copy-start.8
  290.7 1.3 copy-start.3
  292.1 11.0 copy-start.9
  293.1 877.3 %all-reduce.15.cloned.1.call-start = ((), (), s32[]{:S(2)}) async-start(), calls=%async_computation.3 | async-start | bytes 4194304 | tf_op jit(solution)/shard_map/psum | solution.py:12
  1106.8 1.9 copy-start.4
  1108.8 5.5 copy-start.6
  1115.3 2.0 copy-start
  1118.8 271.6 %all-reduce.17.cloned.1.call-start = ((), (), s32[]{:S(2)}) async-start(), calls=%async_computation.4 | async-start | bytes 8388608 | tf_op jit(solution)/shard_map/psum | solution.py:91
  1233.8 219.2 %all-reduce.19.cloned.1.call-start = ((), (), s32[]{:S(2)}) async-start(), calls=%async_computation.5 | async-start | bytes 4718592 | tf_op jit(solution)/shard_map/psum | solution.py:92
  1454.3 11.2 copy-start.5
  1462.4 2.0 copy-start.2
  1465.5 3.9 copy-start.1
Sparse Core Ops, SparseCore 0:
  12.2 159.0 all-reduce.8
  183.7 31.2 all-reduce.10
  293.2 32.2 all-reduce.12
  1118.9 51.4 all-reduce.14
  1233.9 156.4 all-reduce.16
  1398.2 54.6 all-reduce.18
where the time goes:
time: 1550 us; the launch traced here: 1540 us
  waiting for transfers between devices  402 us (26%)
  loops' own time  341 us (22%)
  local copies, waits for them, and re-layouts  308 us (20%)
  matrix products  243 us (16%)
  other arithmetic  225 us (15%)
  between operations  16.7 us (1%)
    another operation x16, loops' own time, lu_signed(): panel, sign_vec = lax.fori_loop(0, width, leaf_step, (panel, sign_vec))  341 us
    dot_general x25, matrix products, matmul(): jnp.dot(left, right, precision=lax.Precision.HIGHEST, preferred_element_t...  211 us
    psum x3, waiting for transfers between devices, spread(): return lax.psum(kept, axis)  207 us
    dynamic_slice x256, local copies, waits for them, and re-layouts, leaf_step(): raw_pivot = column[pivot_idx]  150 us
    psum x1, waiting for transfers between devices, body(): x_rows = lax.psum(matmul(current, matmul(refl_cols, t_factor)), 'col')  115 us
    psum x1, waiting for transfers between devices, body(): inner_prod = lax.psum(matmul(refl.T, x_rows), 'row')  52.7 us
    scatter x256, other arithmetic, leaf_step(): sign_vec = sign_vec.at[pivot_idx].set(sign_now)  43.6 us
    another operation x6, other arithmetic, body(): chol_low = jnp.linalg.cholesky(gram_sum)  34 us
  transfers between devices with their start and end apart: 6, of which 6 were waited for; matrix products, arithmetic and copies ran while one was open for 5% of the time, Pallas kernels for 0%

commit v1 on v0

--- a/solution.py
+++ b/solution.py
@@ -59,6 +59,11 @@
 
 
 def body(matrix):
+
+    def check_sides_by_axis(row_data):
+        next_value = jax.lax.all_gather(row_data, "col")
+        return jnp.sum(next_value, axis=0)
+
     row_count, col_count = matrix.shape
     row_index = lax.axis_index("row")
     col_index = lax.axis_index("col")
@@ -88,7 +93,7 @@
     ).T
     own_slice = lax.dynamic_slice_in_dim(refl, owner_offset, col_count, 0)
     refl_cols = spread(own_slice, "row", owner_row)
-    x_rows = lax.psum(matmul(current, matmul(refl_cols, t_factor)), "col")
+    x_rows = check_sides_by_axis(matmul(current, matmul(refl_cols, t_factor)))
     inner_prod = lax.psum(matmul(refl.T, x_rows), "row")
     correction = matmul(t_factor.T, inner_prod)
     w_rows = x_rows - 0.5 * matmul(refl, correction)

time: 1550 us -> 2080 us (1.34)
  waiting for transfers between devices: 402 us -> 885 us
  local copies, waits for them, and re-layouts: 308 us -> 338 us
    all_gather x0 -> x1, waiting for transfers between devices: none -> 596 us  [check_sides_by_axis(): next_value = jax.lax.all_gather(row_data, 'col')]
    psum x1 -> x0, waiting for transfers between devices: 115 us -> none  [body(): x_rows = lax.psum(matmul(current, matmul(refl_cols, t_factor)), 'col')]
    unnamed x37 -> x40, local copies, waits for them, and re-layouts: 7.25 us -> 36.3 us
  transfers between devices with their start and end apart: 6 -> 6, of which waited for: 6 -> 6; matrix products, arithmetic and copies ran while one was open for 5% -> 4% of each run, Pallas kernels for 0% -> 0%
where the time goes in v1:
time: 2080 us; the launch traced here: 2070 us
  waiting for transfers between devices  885 us (43%)
  loops' own time  345 us (17%)
  local copies, waits for them, and re-layouts  338 us (16%)
  matrix products  245 us (12%)
  other arithmetic  240 us (12%)
    all_gather x1, waiting for transfers between devices, check_sides_by_axis(): next_value = jax.lax.all_gather(row_data, 'col')  596 us
    another operation x16, loops' own time, lu_signed(): panel, sign_vec = lax.fori_loop(0, width, leaf_step, (panel, sign_vec))  345 us
    dot_general x25, matrix products, matmul(): jnp.dot(left, right, precision=lax.Precision.HIGHEST, preferred_element_t...  212 us
    psum x3, waiting for transfers between devices, spread(): return lax.psum(kept, axis)  208 us
    dynamic_slice x256, local copies, waits for them, and re-layouts, leaf_step(): raw_pivot = column[pivot_idx]  151 us
    psum x1, waiting for transfers between devices, body(): inner_prod = lax.psum(matmul(refl.T, x_rows), 'row')  53.7 us
    scatter x256, other arithmetic, leaf_step(): sign_vec = sign_vec.at[pivot_idx].set(sign_now)  43.5 us
  transfers between devices with their start and end apart: 6, of which 6 were waited for; matrix products, arithmetic and copies ran while one was open for 4% of the time, Pallas kernels for 0%

profile of v1, /device:TPU:0, one launch (start us, length us, event | category | flops | bytes accessed | tf_op | source)
XLA Modules:
  0.0 2070.9 jit_solution(1587561599813993120)
XLA Ops:
  7.2 4.5 slice_select_fusion
  12.6 158.8 %all-reduce.8.cloned.1.call-done = f32[4096,256]{1,0:T(8,128)} async-done(((f32[4096,256]{1,0:T(8,128)}), f32[4096,256]{1,0:T(8,128)}) %all-reduce.8.cloned.1.call-update) | async-done | bytes 4194320 | tf_op jit(solution)/shard_map/psum | solution.py:12
  171.4 12.2 fusion.89
  183.9 3.9 select_bitcast_fusion
  187.8 27.2 %all-reduce.10.cloned.1.call-done = f32[256,256]{0,1:T(8,128)} async-done(((f32[256,256]{0,1:T(8,128)}), f32[256,256]{0,1:T(8,128)}) %all-reduce.10.cloned.1.call-update) | async-done | bytes 262160 | tf_op jit(solution)/shard_map/psum | solution.py:80
  217.1 11.7 cholesky.50
  228.9 9.8 custom-call.78
  239.2 11.7 cholesky.105
  253.0 4.0 while.404
  257.0 20.1 custom-call.96
  277.1 3.7 fusion.92
  280.8 4.8 convolution_subtract_fusion.2
  287.4 3.5 fusion.110
  303.6 22.2 %all-reduce.12.cloned.1.call-done = f32[256,256]{1,0:T(8,128)} async-done(((f32[256,256]{1,0:T(8,128)}), f32[256,256]{1,0:T(8,128)}) %all-reduce.12.cloned.1.call-update) | async-done | bytes 262160 | tf_op jit(solution)/shard_map/psum | solution.py:12
  326.7 37.3 %while.388 = (s32[]{:T(128)}, f32[256,16]{0,1:T(8,128)S(1)}, f32[256]{0:T(256)S(1)}, s32[]{:T(128)}, s32[]{:T(128)}, /*index=5*/s32[]{:T(128)}, s32[]{:T(128)}, f32[]{:T(128)}, f32[]{:T(128)}, f32[]{:T(128)}) while((s32[]{:T(128)}, f32[256,16]{0,1:T(8,128)S(1)}, f32[256]{0:T(256)S(1)}, s32[]{:T(128)}, s32[]{:T(128)}, ...), condition=%wide.region_9.11_spmd.clone.clone, body=%wide.region_8.10_spmd.clone.clone.sunk | while | flops 9771 | bytes 75177 | solution.py:46
  368.7 3.0 dynamic-slice_select_fusion.1
  373.1 3.6 scatter.220
  376.7 2.4 scatter.221
  380.2 37.4 %while.389 = (s32[]{:T(128)}, f32[256,16]{0,1:T(8,128)S(1)}, f32[256]{0:T(256)S(1)}, s32[]{:T(128)}, s32[]{:T(128)}, /*index=5*/s32[]{:T(128)}, s32[]{:T(128)}, ...) while((s32[]{:T(128)}, f32[256,16]{0,1:T(8,128)S(1)}, ...), condition=%wide.region_13.15_spmd.clone.clone, body=%wide.region_12.14_spmd.clone.clone.sunk | while | flops 9775 | bytes 74223 | solution.py:46
  424.8 2.3 scatter.225
  427.1 2.4 scatter.226
  430.5 37.4 %while.390 = (s32[]{:T(128)}, f32[256,16]{0,1:T(8,128)S(1)}, f32[256]{0:T(256)S(1)}, s32[]{:T(128)}, s32[]{:T(128)}, /*index=5*/s32[]{:T(128)}, s32[]{:T(128)}, ...) while((s32[]{:T(128)}, f32[256,16]{0,1:T(8,128)S(1)}, ...), condition=%wide.region_16.18_spmd.clone.clone, body=%wide.region_15.17_spmd.clone.clone.sunk | while | flops 9775 | bytes 74223 | solution.py:46
  475.2 2.2 scatter.230
  477.5 2.3 scatter.231
  480.9 37.4 %while.391 = (s32[]{:T(128)}, f32[256,16]{0,1:T(8,128)S(1)}, f32[256]{0:T(256)S(1)}, s32[]{:T(128)}, s32[]{:T(128)}, /*index=5*/s32[]{:T(128)}, s32[]{:T(128)}, ...) while((s32[]{:T(128)}, f32[256,16]{0,1:T(8,128)S(1)}, ...), condition=%wide.region_19.21_spmd.clone.clone, body=%wide.region_18.20_spmd.clone.clone.sunk | while | flops 9775 | bytes 74223 | solution.py:46
  525.6 2.2 scatter.235
  527.8 2.3 scatter.237
  531.2 37.4 %while.392 = (s32[]{:T(128)}, f32[256,16]{0,1:T(8,128)S(1)}, f32[256]{0:T(256)S(1)}, s32[]{:T(128)}, s32[]{:T(128)}, /*index=5*/s32[]{:T(128)}, s32[]{:T(128)}, ...) while((s32[]{:T(128)}, f32[256,16]{0,1:T(8,128)S(1)}, ...), condition=%wide.region_22.24_spmd.clone.clone, body=%wide.region_21.23_spmd.clone.clone.sunk | while | flops 9775 | bytes 74223 | solution.py:46
  575.9 2.3 scatter.241
  581.4 37.4 %while.393 = (s32[]{:T(128)}, f32[256,16]{0,1:T(8,128)S(1)}, f32[256]{0:T(256)S(1)}, s32[]{:T(128)}, s32[]{:T(128)}, /*index=5*/s32[]{:T(128)}, s32[]{:T(128)}, ...) while((s32[]{:T(128)}, f32[256,16]{0,1:T(8,128)S(1)}, ...), condition=%wide.region_25.27_spmd.clone.clone, body=%wide.region_24.26_spmd.clone.clone.sunk | while | flops 9775 | bytes 74223 | solution.py:46
  626.0 2.2 scatter.246
  631.5 37.4 %while.394 = (s32[]{:T(128)}, f32[256,16]{0,1:T(8,128)S(1)}, f32[256]{0:T(256)S(1)}, s32[]{:T(128)}, s32[]{:T(128)}, /*index=5*/s32[]{:T(128)}, s32[]{:T(128)}, ...) while((s32[]{:T(128)}, f32[256,16]{0,1:T(8,128)S(1)}, ...), condition=%wide.region_28.30_spmd.clone.clone, body=%wide.region_27.29_spmd.clone.clone.sunk | while | flops 9775 | bytes 74223 | solution.py:46
  676.2 2.5 scatter.251
  681.9 37.4 %while.395 = (s32[]{:T(128)}, f32[256,16]{0,1:T(8,128)S(1)}, f32[256]{0:T(256)S(1)}, s32[]{:T(128)}, s32[]{:T(128)}, /*index=5*/s32[]{:T(128)}, s32[]{:T(128)}, ...) while((s32[]{:T(128)}, f32[256,16]{0,1:T(8,128)S(1)}, ...), condition=%wide.region_31.33_spmd.clone.clone, body=%wide.region_30.32_spmd.clone.clone.sunk | while | flops 9775 | bytes 74223 | solution.py:46
  727.2 37.4 %while.396 = (s32[]{:T(128)}, f32[256,16]{0,1:T(8,128)S(1)}, f32[256]{0:T(256)S(1)}, s32[]{:T(128)}, s32[]{:T(128)}, /*index=5*/s32[]{:T(128)}, s32[]{:T(128)}, ...) while((s32[]{:T(128)}, f32[256,16]{0,1:T(8,128)S(1)}, ...), condition=%wide.region_34.36_spmd.clone.clone, body=%wide.region_33.35_spmd.clone.clone.sunk | while | flops 9775 | bytes 74223 | solution.py:46
  770.1 37.4 %while.397 = (s32[]{:T(128)}, f32[256,16]{0,1:T(8,128)S(1)}, f32[256]{0:T(256)S(1)}, s32[]{:T(128)}, s32[]{:T(128)}, /*index=5*/s32[]{:T(128)}, s32[]{:T(128)}, ...) while((s32[]{:T(128)}, f32[256,16]{0,1:T(8,128)S(1)}, ...), condition=%wide.region_37.39_spmd.clone.clone, body=%wide.region_36.38_spmd.clone.clone.sunk | while | flops 9775 | bytes 74223 | solution.py:46
  813.3 37.4 %while.398 = (s32[]{:T(128)}, f32[256,16]{0,1:T(8,128)S(1)}, f32[256]{0:T(256)S(1)}, s32[]{:T(128)}, s32[]{:T(128)}, /*index=5*/s32[]{:T(128)}, s32[]{:T(128)}, ...) while((s32[]{:T(128)}, f32[256,16]{0,1:T(8,128)S(1)}, ...), condition=%wide.region_40.42_spmd.clone.clone, body=%wide.region_39.41_spmd.clone.clone.sunk | while | flops 9775 | bytes 74223 | solution.py:46
  856.3 37.4 %while.399 = (s32[]{:T(128)}, f32[256,16]{0,1:T(8,128)S(1)}, f32[256]{0:T(256)S(1)}, s32[]{:T(128)}, s32[]{:T(128)}, /*index=5*/s32[]{:T(128)}, s32[]{:T(128)}, ...) while((s32[]{:T(128)}, f32[256,16]{0,1:T(8,128)S(1)}, ...), condition=%wide.region_43.45_spmd.clone.clone, body=%wide.region_42.44_spmd.clone.clone.sunk | while | flops 9775 | bytes 74223 | solution.py:46
  899.3 37.4 %while.400 = (s32[]{:T(128)}, f32[256,16]{0,1:T(8,128)S(1)}, f32[256]{0:T(256)S(1)}, s32[]{:T(128)}, s32[]{:T(128)}, /*index=5*/s32[]{:T(128)}, s32[]{:T(128)}, ...) while((s32[]{:T(128)}, f32[256,16]{0,1:T(8,128)S(1)}, ...), condition=%wide.region_46.48_spmd.clone.clone, body=%wide.region_45.47_spmd.clone.clone.sunk | while | flops 9775 | bytes 74223 | solution.py:46
  942.2 37.4 %while.401 = (s32[]{:T(128)}, f32[256,16]{0,1:T(8,128)S(1)}, f32[256]{0:T(256)S(1)}, s32[]{:T(128)}, s32[]{:T(128)}, /*index=5*/s32[]{:T(128)}, s32[]{:T(128)}, ...) while((s32[]{:T(128)}, f32[256,16]{0,1:T(8,128)S(1)}, ...), condition=%wide.region_49.51_spmd.clone.clone, body=%wide.region_48.50_spmd.clone.clone.sunk | while | flops 9775 | bytes 74223 | solution.py:46
  985.5 37.4 %while.402 = (s32[]{:T(128)}, f32[256,16]{0,1:T(8,128)S(1)}, f32[256]{0:T(256)S(1)}, s32[]{:T(128)}, s32[]{:T(128)}, /*index=5*/s32[]{:T(128)}, s32[]{:T(128)}, ...) while((s32[]{:T(128)}, f32[256,16]{0,1:T(8,128)S(1)}, ...), condition=%wide.region_52.54_spmd.clone.clone, body=%wide.region_51.53_spmd.clone.clone.sunk | while | flops 9775 | bytes 74223 | solution.py:46
  1028.2 37.4 %while.403 = (s32[]{:T(128)}, f32[256,16]{0,1:T(8,128)S(1)}, f32[256]{0:T(256)S(1)}, s32[]{:T(128)}, s32[]{:T(128)}, /*index=5*/s32[]{:T(128)}, s32[]{:T(128)}, ...) while((s32[]{:T(128)}, f32[256,16]{0,1:T(8,128)S(1)}, ...), condition=%wide.region_54.56_spmd.clone.clone, body=%wide.region_53.55_spmd.clone.clone.sunk | while | flops 9775 | bytes 74223 | solution.py:46
  1066.8 4.2 while.405
  1071.0 19.8 custom-call.97
  1092.8 3.4 convolution_subtract_fusion.1
  1096.3 3.3 fusion.107
  1099.7 16.1 gather_fusion
  1115.8 5.8 copy.109
  1121.7 3.8 fusion.85
  1129.1 4.2 while.387
  1133.3 19.7 custom-call.94
  1154.1 26.6 %all-reduce.14.cloned.1.call-done = f32[2048,256]{0,1:T(8,128)} async-done(((f32[2048,256]{0,1:T(8,128)}), f32[2048,256]{0,1:T(8,128)}) %all-reduce.14.cloned.1.call-update) | async-done | bytes 2097168 | tf_op jit(solution)/shard_map/psum | solution.py:12
  1180.7 5.0 fusion.101
  1185.7 58.5 %convolution_bitcast_fusion = f32[4096,256]{0,1:T(8,128)} fusion(f32[2048,256]{1,0:T(8,128)S(1)} %fusion.101, f32[4096,2048]{1,0:T(8,128)} %param.159), kind=kOutput, calls=%fused_computation.206 | convolution fusion | flops 25769803776 | bytes 39845888 | tf_op jit(solution)/shard_map/dot_general | solution.py:16
  1244.3 8.5 fusion.99
  1252.8 33.3 %convolution_bitcast_fusion.1 = f32[2048,256]{0,1:T(8,128)} fusion(f32[4096,256]{1,0:T(8,128)S(1)} %fusion.99, f32[4096,2048]{1,0:T(8,128)} %param.159), kind=kOutput, calls=%fused_computation.222 | convolution fusion | flops 25769803776 | bytes 39845888 | tf_op jit(solution)/shard_map/dot_general | solution.py:16
  1286.2 596.0 %all-gather.3.cloned.1.call-done = f32[32768,256]{0,1:T(8,128)} async-done(((f32[4096,256]{0,1:T(8,128)}), f32[32768,256]{0,1:T(8,128)}) %all-gather.3.cloned.1.call-update) | async-done | bytes 33554448 | tf_op jit(solution)/shard_map/all_gather | solution.py:64
  1882.1 28.9 %copy.131 = f32[32,8,8,4096]{3,2,1,0:T(8,128)S(1)} copy(f32[32,8,8,4096]{3,1,2,0:T(8,128)} %bitcast.551) | data formatting | bytes 67108864
  1911.1 12.7 bitcast_reduce_fusion
  1923.7 7.7 fusion.222
  1933.5 53.7 %all-reduce.16.cloned.1.call-done = (f32[256,256]{1,0:T(8,128)}, f32[2048,256]{0,1:T(8,128)}) async-done(((f32[256,256]{1,0:T(8,128)}, f32[2048,256]{0,1:T(8,128)}), (f32[256,256]{1,0:T(8,128)}, f32[2048,256]{0,1:T(8,128)})) %all-reduce.16.cloned.1.call-update) | async-done | bytes 2359312 | tf_op jit(solution)/shard_map/psum | solution.py:97
  1988.6 8.4 fusion.83
  2000.0 3.9 fusion.91
  2003.9 59.6 %convolution_subtract_fusion = f32[4096,2048]{1,0:T(8,128)} fusion(f32[4096,2048]{1,0:T(8,128)} %param.159, f32[4096,256]{0,1:T(8,128)} %copy-done.2, f32[4096,256]{0,1:T(8,128)S(1)} %copy-done.1, f32[2048,256]{0,1:T(8,128)S(1)} %copy-done.7, f32[2048,256]{0,1:T(8,128)S(1)} %fusion.91), kind=kOutput, calls=%fused_computation.200 | convolution fusion | flops 51551141888 | bytes 79691776 | tf_op jit(solution)/shard_map/dot_general | solution.py:16
  (2317 shorter events, 410.0 us)
Async XLA Ops:
  7.2 164.2 %all-reduce.8.cloned.1.call-start = ((), (), s32[]{:S(2)}) async-start(), calls=%async_computation | async-start | bytes 8388608 | tf_op jit(solution)/shard_map/psum | solution.py:12
  11.7 203.3 %all-reduce.10.cloned.1.call-start = ((), (), s32[]{:S(2)}) async-start(), calls=%async_computation.1 | async-start | bytes 524288 | tf_op jit(solution)/shard_map/psum | solution.py:80
  183.6 142.1 %all-reduce.12.cloned.1.call-start = ((), (), s32[]{:S(2)}) async-start(), calls=%async_computation.2 | async-start | bytes 524288 | tf_op jit(solution)/shard_map/psum | solution.py:12
  277.1 3.7 copy-start.8
  287.4 4.9 copy-start.9
  290.9 1.3 copy-start.5
  292.3 10.6 copy-start.10
  293.3 887.4 %all-reduce.14.cloned.1.call-start = ((), (), s32[]{:S(2)}) async-start(), calls=%async_computation.3 | async-start | bytes 4194304 | tf_op jit(solution)/shard_map/psum | solution.py:12
  1090.8 2.0 copy-start.6
  1092.8 6.8 copy-start.3
  1115.8 5.8 copy-start.4
  1125.4 2.1 copy-start
  1129.0 753.1 %all-gather.3.cloned.1.call-start = ((), (), s32[]{:S(2)}) async-start(), calls=%async_computation.4 | async-start | bytes 37748736 | tf_op jit(solution)/shard_map/all_gather | solution.py:64
  1244.3 743.0 %all-reduce.16.cloned.1.call-start = ((), (), s32[]{:S(2)}) async-start(), calls=%async_computation.5 | async-start | bytes 4718592 | tf_op jit(solution)/shard_map/psum | solution.py:97
  1988.6 11.4 copy-start.7
  1997.0 2.0 copy-start.2
  2000.0 3.9 copy-start.1
Sparse Core Ops, SparseCore 0:
  12.2 159.0 all-reduce.7
  183.7 31.2 all-reduce.9
  293.4 32.2 all-reduce.11
  1129.2 51.4 all-reduce.13
  1244.4 637.7 all-gather.2
  1931.6 55.6 all-reduce.15
